TPU v7x, 32 devices: a whole 2x2x4 slice. The times are simulated.
32 devices in a mesh: recv: 4 (over x, core), send: 8 (over z, y).
Axes of the slice: x: 2, y: 2, z: 4, core: 2. Of those that a mesh axis runs over, the one named last changes fastest.
Arguments:
- latent: float32 [4096, 512], P(('recv', 'send')), may hold values from -6 to 6
- edge_feat: float32 [32768, 512], P(('recv', 'send')), may hold values from -6 to 6
- senders: int32 [32768], P(('recv', 'send')), may hold values from 0 to 4095, as said below
- receivers: int32 [32768], P(('recv', 'send')), may hold values from 0 to 4095, as said below
- live_blocks: int32 [32], P(('recv', 'send')), may hold values from 1 to 8, as said below
- cotangent: float32 [32768, 512], P(('recv', 'send')), may hold values from -6 to 6
- w_first: float32 [1536, 512], replicated, may hold values from -0.15625 to 0.15625
- first_bias: float32 [512], replicated, may hold values from -3 to 3
- w_second: float32 [512, 512], replicated, may hold values from -0.25 to 0.25
- second_bias: float32 [512], replicated, may hold values from -3 to 3
- norm_gain: float32 [512], replicated, may hold values from 0.1 to 1.9
Outputs:
- edge_grad: float32 [32768, 512], P(('recv', 'send'))
- sender_grad: float32 [4096, 512], P(('recv', 'send'))
- receiver_grad: float32 [4096, 512], P(('recv', 'send'))
- first_weight_grad: float32 [1536, 512], replicated
- second_weight_grad: float32 [512, 512], replicated
- bias_grads: float32 [4, 512], replicated
Inputs may be any that keep to these rules, and one draw needn't show every extreme that they name: `receivers`: slot e lies in tile t = e // 1024; with i = t // (devices along send), its receiver r has (r // 128) // (devices along send) = i. The first two slots of every tile name the last and the first node of that receiver block. `senders`: slot e lies in tile t = e // 1024; with j = t mod (devices along send), its sender s has (s // 128) mod (devices along send) = j. The first two slots of every tile name the last and the first node of that sender block. Tile t's first 128 * live_blocks[t] slots hold edges; its other slots are padding whose cotangent is ignored. Some tile is full in every draw.
All inputs are finite; a program needn't handle non-finite values.
Results may differ from a plain program's by a relative error of at most 0.0001.
Values sent between devices are 32-bit elements; how exact they have to be, the bound alone decides.
A program may use at most 128 MiB of HBM per device.

v0:
```python
import math
import jax
import jax.numpy as jnp
from jax import lax
from jax.sharding import PartitionSpec as P

norm_eps = 1e-05
block_rows = 128


def exact_dot(left, right):
    return jnp.dot(left, right, precision=lax.Precision.HIGHEST, preferred_element_type=jnp.float32)


def outer_sum(left, right):
    return lax.dot_general(
        left,
        right,
        (((0,), (0,)), ((), ())),
        precision=lax.Precision.HIGHEST,
        preferred_element_type=jnp.float32,
    )


def trans_dot(left, right):
    return lax.dot_general(
        left,
        right,
        (((1,), (1,)), ((), ())),
        precision=lax.Precision.HIGHEST,
        preferred_element_type=jnp.float32,
    )


def shards(
    latent,
    edge_feat,
    senders,
    receivers,
    live_blocks,
    cotangent,
    w_first,
    first_bias,
    w_second,
    second_bias,
    norm_gain,
):
    model_width = latent.shape[1]
    node_rows = latent.shape[0]
    slot_count = edge_feat.shape[0]
    recv_count = lax.axis_size("recv")
    send_count = lax.axis_size("send")
    recv_index = lax.axis_index("recv")
    recv_local = receivers - recv_index * (send_count * node_rows)
    piece_index = senders // node_rows
    send_local = piece_index // send_count * node_rows + senders % node_rows
    live_limit = block_rows * live_blocks[0]
    sender_table = lax.all_gather(latent, "recv", axis=0, tiled=True)
    receiver_table = lax.all_gather(latent, "send", axis=0, tiled=True)
    first_rows = 3 * model_width

    def block_work(accs, edge_rows, grad_rows, sender_rows, recv_ids):
        first_grad, second_grad, hidden_bias, outer_bias, gain_grad, offset_grad, receiver_acc = (
            accs
        )
        receiver_rows = jnp.take(receiver_table, recv_ids, axis=0)
        joined = jnp.concatenate([edge_rows, sender_rows, receiver_rows], axis=1)
        hidden = exact_dot(joined, w_first) + first_bias
        sigmoid_hidden = jax.nn.sigmoid(hidden)
        active = hidden * sigmoid_hidden
        output = exact_dot(active, w_second) + second_bias
        centred = output - jnp.mean(output, axis=1, keepdims=True)
        inv_std = lax.rsqrt(jnp.mean(centred * centred, axis=1, keepdims=True) + norm_eps)
        normed = centred * inv_std
        scaled = grad_rows * norm_gain
        norm_grad = inv_std * (
            scaled
            - jnp.mean(scaled, axis=1, keepdims=True)
            - normed * jnp.mean(scaled * normed, axis=1, keepdims=True)
        )
        hidden_grad = (
            trans_dot(norm_grad, w_second)
            * sigmoid_hidden
            * (1.0 + hidden * (1.0 - sigmoid_hidden))
        )
        first_grad = first_grad + outer_sum(joined, hidden_grad)
        second_grad = second_grad + outer_sum(active, norm_grad)
        hidden_bias = hidden_bias + jnp.sum(hidden_grad, axis=0)
        outer_bias = outer_bias + jnp.sum(norm_grad, axis=0)
        gain_grad = gain_grad + jnp.sum(grad_rows * normed, axis=0)
        offset_grad = offset_grad + jnp.sum(grad_rows, axis=0)
        joined_grad = trans_dot(hidden_grad, w_first)
        edge_part = joined_grad[:, :model_width]
        sender_part = joined_grad[:, model_width : 2 * model_width]
        receiver_acc = receiver_acc.at[recv_ids].add(joined_grad[:, 2 * model_width :])
        accs = (
            first_grad,
            second_grad,
            hidden_bias,
            outer_bias,
            gain_grad,
            offset_grad,
            receiver_acc,
        )
        return (accs, grad_rows + edge_part, sender_part)

    def local_block(offset):
        edge_rows = lax.dynamic_slice_in_dim(edge_feat, offset, block_rows, 0)
        position = offset + jnp.arange(block_rows, dtype=jnp.int32)
        live_rows = (position < live_limit).astype(jnp.float32)[:, None]
        grad_rows = lax.dynamic_slice_in_dim(cotangent, offset, block_rows, 0) * live_rows
        send_ids = lax.dynamic_slice_in_dim(send_local, offset, block_rows, 0)
        recv_ids = lax.dynamic_slice_in_dim(recv_local, offset, block_rows, 0)
        sender_rows = jnp.take(sender_table, send_ids, axis=0)
        return (edge_rows, grad_rows, send_ids, recv_ids, sender_rows)

    feature_zeros = jnp.zeros((model_width,), jnp.float32)
    accs = (
        jnp.zeros((first_rows, model_width), jnp.float32),
        jnp.zeros((model_width, model_width), jnp.float32),
        feature_zeros,
        feature_zeros,
        feature_zeros,
        feature_zeros,
        jnp.zeros(receiver_table.shape, jnp.float32),
    )
    sender_acc = jnp.zeros(sender_table.shape, jnp.float32)
    edge_out = jnp.zeros(edge_feat.shape, jnp.float32)

    def own_step(block, carried):
        accs_now, sender_now, edge_now = carried
        offset = block * block_rows
        edge_rows, grad_rows, send_ids, recv_ids, sender_rows = local_block(offset)
        accs_now, edge_block, sender_block = block_work(
            accs_now, edge_rows, grad_rows, sender_rows, recv_ids
        )
        sender_now = sender_now.at[send_ids].add(sender_block)
        edge_now = lax.dynamic_update_slice_in_dim(edge_now, edge_block, offset, 0)
        return (accs_now, sender_now, edge_now)

    accs, sender_acc, edge_out = lax.fori_loop(
        0, live_blocks[0], own_step, (accs, sender_acc, edge_out)
    )
    first_grad, second_grad, hidden_bias, outer_bias, gain_grad, offset_grad, receiver_acc = accs
    sender_grad = lax.psum_scatter(sender_acc, "recv", scatter_dimension=0, tiled=True)
    receiver_grad = lax.psum_scatter(receiver_acc, "send", scatter_dimension=0, tiled=True)
    small_grads = jnp.stack([hidden_bias, outer_bias, gain_grad, offset_grad])
    first_total, second_total, small_total = lax.psum(
        (first_grad, second_grad, small_grads), ("recv", "send")
    )
    factor = 1.0 / math.sqrt(slot_count * recv_count * send_count)
    return (
        edge_out,
        sender_grad,
        receiver_grad,
        first_total * factor,
        second_total * factor,
        small_total * factor,
    )


def solution(mesh):
    return jax.shard_map(
        shards,
        mesh=mesh,
        in_specs=(
            P(("recv", "send"), None),
            P(("recv", "send"), None),
            P(("recv", "send")),
            P(("recv", "send")),
            P(("recv", "send")),
            P(("recv", "send"), None),
            P(),
            P(),
            P(),
            P(),
            P(),
        ),
        out_specs=(
            P(("recv", "send"), None),
            P(("recv", "send"), None),
            P(("recv", "send"), None),
            P(),
            P(),
            P(),
        ),
        check_vma=False,
    )
```

profile of v0, /device:TPU:0, one launch (start us, length us, event | category | flops | bytes accessed | tf_op | source)
XLA Modules:
  0.0 650.2 jit_solution(7967292514408695948)
XLA Ops:
  7.2 0.7 all-gather.3.cloned.1.call-update
  7.9 0.7 all-gather.5.cloned.1.call-update
  9.3 0.7 fusion.16
  10.1 18.9 %all-gather.3.cloned.1.call-done = f32[512,512]{1,0:T(8,128)} async-done(((f32[128,512]{1,0:T(8,128)}), f32[512,512]{1,0:T(8,128)}) %all-gather.3.cloned.1.call-update) | async-done | bytes 1048592 | tf_op jit(solution)/shard_map/all_gather | solution.py:58
  29.0 51.5 %all-gather.5.cloned.1.call-done = f32[1024,512]{1,0:T(8,128)} async-done(((f32[128,512]{1,0:T(8,128)}), f32[1024,512]{1,0:T(8,128)}) %all-gather.5.cloned.1.call-update) | async-done | bytes 2097168 | tf_op jit(solution)/shard_map/all_gather | solution.py:59
  80.5 1.1 broadcast.80.clone
  81.6 1.1 broadcast.80
  82.7 1.6 broadcast.81.clone
  84.3 1.6 broadcast.81
  86.0 2.1 broadcast_in_dim.38
  88.0 1.0 copy-done
  89.0 79.1 %while.26 = (s32[]{:T(128)}, f32[1536,512]{1,0:T(8,128)}, f32[512,512]{1,0:T(8,128)}, f32[512]{0:T(512)S(1)}, f32[512]{0:T(512)S(1)}, /*index=5*/f32[512]{0:T(51...) while((s32[]{:T(128)}, f32[1536,512]{1,0:T(8,128)}, ...), condition=%wide.region_11.12_spmd, body=%wide.region_0.11_spmd.sunk | while | flops 4836823040 | bytes 37814700 | solution.py:141
  89.8 3.2 gather_fusion
  93.0 1.0 broadcast_select_fusion.4
  94.0 2.9 gather_fusion.1
  96.9 1.1 broadcast_select_fusion.5
  98.1 1.9 convolution_add_fusion.7
  100.0 0.8 fusion.59
  101.0 1.2 multiply_reduce_fusion.7
  102.3 1.1 fusion.60
  103.4 1.2 fusion.61
  104.7 3.2 convolution_add_fusion.9
  107.9 4.2 fusion.62
  112.1 4.0 scatter_custom_fusion.11
  116.1 1.8 fusion.63
  117.9 4.7 scatter_custom_fusion.10
  122.6 5.6 convolution_add_fusion.8
  129.1 3.2 gather_fusion
  132.2 1.0 broadcast_select_fusion.4
  133.3 2.9 gather_fusion.1
  136.2 1.1 broadcast_select_fusion.5
  137.3 1.9 convolution_add_fusion.7
  139.2 0.8 fusion.59
  140.3 1.2 multiply_reduce_fusion.7
  141.5 1.1 fusion.60
  142.7 1.2 fusion.61
  143.9 3.2 convolution_add_fusion.9
  147.1 4.2 fusion.62
  151.4 4.0 scatter_custom_fusion.11
  155.3 1.8 fusion.63
  157.1 4.7 scatter_custom_fusion.10
  161.8 5.6 convolution_add_fusion.8
  169.3 274.5 %psum.23 = f32[4,512]{1,0:T(4,128)S(1)} all-reduce(f32[4,512]{1,0:T(4,128)S(1)} %pad_maximum_fusion.3), channel_id=1, replica_groups=mesh['recv'=4,'send'=8] {'recv','send'}, use_global_device_ids=true, to_apply=%region_16.17 | all-reduce | flops 2048 | bytes 16384 | tf_op jit(solution)/shard_map/psum | solution.py:148
  444.4 100.4 %all-reduce.3.cloned.1.call-done = (f32[1536,512]{1,0:T(8,128)}, f32[512,512]{1,0:T(8,128)}) async-done(((f32[1536,512]{1,0:T(8,128)}, f32[512,512]{1,0:T(8,128)}), (f32[1536,512]{1,0:T(8,128)}, f32[512,512]{1,0:T(8,128)})) %all-reduce.3.cloned.1.call-update) | async-done | bytes 4194320 | tf_op jit(solution)/shard_map/psum | solution.py:148
  544.8 2.3 broadcast_multiply_fusion.4
  547.1 3.9 broadcast_multiply_fusion.3
  551.0 20.5 %reduce-scatter.3.cloned.1.call-done = f32[128,512]{1,0:T(8,128)} async-done(((f32[512,512]{1,0:T(8,128)}), f32[128,512]{1,0:T(8,128)}) %reduce-scatter.3.cloned.1.call-update) | async-done | bytes 262160 | tf_op jit(solution)/shard_map/reduce_scatter | solution.py:145
  571.6 72.1 %reduce-scatter.5.cloned.1.call-done = f32[128,512]{1,0:T(8,128)} async-done(((f32[1024,512]{1,0:T(8,128)}), f32[128,512]{1,0:T(8,128)}) %reduce-scatter.5.cloned.1.call-update) | async-done | bytes 262160 | tf_op jit(solution)/shard_map/reduce_scatter | solution.py:146
  (63 shorter events, 2.8 us)
Async XLA Ops:
  7.2 21.8 %all-gather.3.cloned.1.call-start = ((), (), s32[]{:S(2)}) async-start(), calls=%async_computation.2 | async-start | bytes 1310720 | tf_op jit(solution)/shard_map/all_gather | solution.py:58
  7.9 72.6 %all-gather.5.cloned.1.call-start = ((), (), s32[]{:S(2)}) async-start(), calls=%async_computation.3 | async-start | bytes 2359296 | tf_op jit(solution)/shard_map/all_gather | solution.py:59
  8.6 536.1 %all-reduce.3.cloned.1.call-start = ((), (), s32[]{:S(2)}) async-start(), calls=%async_computation.6 | async-start | bytes 8388608 | tf_op jit(solution)/shard_map/psum | solution.py:148
  84.3 3.7 copy-start.5
  84.3 3.7 copy-start.6
  84.3 3.7 copy-start.7
  86.0 3.0 copy-start
  94.0 5.9 copy-start.2
  98.1 1.9 copy-start.3
  98.1 1.9 copy-start.4
  98.1 1.9 copy-start.1
  133.3 5.9 copy-start.2
  137.3 1.9 copy-start.3
  137.3 1.9 copy-start.4
  137.3 1.9 copy-start.1
  168.1 403.5 %reduce-scatter.3.cloned.1.call-start = ((), (), s32[]{:S(2)}) async-start(), calls=%async_computation.4 | async-start | bytes 1310720 | tf_op jit(solution)/shard_map/reduce_scatter | solution.py:145
  168.7 475.0 %reduce-scatter.5.cloned.1.call-start = ((), (), s32[]{:S(2)}) async-start(), calls=%async_computation.5 | async-start | bytes 2359296 | tf_op jit(solution)/shard_map/reduce_scatter | solution.py:146
Sparse Core Ops, SparseCore 0:
  9.6 19.4 all-gather.2
  31.1 49.2 all-gather.4
  168.2 376.5 all-reduce.2
  547.8 23.7 reduce-scatter.2
  576.0 67.7 reduce-scatter.4
where the time goes:
time: 654 us; the launch traced here: 650 us
  blocking collectives  275 us (42%)
  waiting for transfers between devices  266 us (41%)
  other arithmetic  38.3 us (6%)
  matrix products  34 us (5%)
  local copies, waits for them, and re-layouts  20.6 us (3%)
  between operations  14.5 us (2%)
    psum x1, blocking collectives, shards(): lax.psum((first_grad, second_grad, small_grads), ('recv', 'send'))  275 us
    psum x1, waiting for transfers between devices, shards(): lax.psum((first_grad, second_grad, small_grads), ('recv', 'send'))  100 us
    reduce_scatter x1, waiting for transfers between devices, shards(): lax.psum_scatter(receiver_acc, 'send', scatter_dimension=0, tiled=True)  72.1 us
    all_gather x1, waiting for transfers between devices, shards(): receiver_table = lax.all_gather(latent, 'send', axis=0, tiled=True)  51.5 us
    reduce_scatter x1, waiting for transfers between devices, shards(): lax.psum_scatter(sender_acc, 'recv', scatter_dimension=0, tiled=True)  20.5 us
    all_gather x1, waiting for transfers between devices, shards(): sender_table = lax.all_gather(latent, 'recv', axis=0, tiled=True)  18.9 us
    dot_general x4, matrix products, outer_sum(): lax.dot_general(left, right, (((0,), (0,)), ((), ())), precision=lax.Prec...  17.7 us
  transfers between devices with their start and end apart: 5, of which 5 were waited for; matrix products, arithmetic and copies ran while one was open for 1% of the time, Pallas kernels for 0%

commit v1 on v0

--- a/solution.py
+++ b/solution.py
@@ -6,6 +6,19 @@
 
 norm_eps = 1e-05
 block_rows = 128
+
+
+def collect(x, axis, dim):
+    ways = lax.axis_size(axis)
+    up = [(d, (d + 1) % ways) for d in range(ways)]
+    down = [(d, (d - 1) % ways) for d in range(ways)]
+    earlier, later = ([x], [x])
+    for _ in range(ways // 2):
+        earlier.append(lax.ppermute(earlier[-1], axis, up))
+    for _ in range((ways - 1) // 2):
+        later.append(lax.ppermute(later[-1], axis, down))
+    line = jnp.concatenate([*earlier[::-1], *later[1:]], axis=dim)
+    return jnp.roll(line, (lax.axis_index(axis) - ways // 2) * x.shape[dim], axis=dim)
 
 
 def exact_dot(left, right):
@@ -56,7 +69,7 @@
     send_local = piece_index // send_count * node_rows + senders % node_rows
     live_limit = block_rows * live_blocks[0]
     sender_table = lax.all_gather(latent, "recv", axis=0, tiled=True)
-    receiver_table = lax.all_gather(latent, "send", axis=0, tiled=True)
+    receiver_table = collect(latent, "send", 0)
     first_rows = 3 * model_width
 
     def block_work(accs, edge_rows, grad_rows, sender_rows, recv_ids):

time: 654 us -> 627 us (0.959)
  waiting for transfers between devices: 266 us -> 219 us
  starting transfers between devices: 0.19 us -> 26 us
    all_gather x1 -> x0, waiting for transfers between devices: 51.5 us -> none  [shards(): receiver_table = lax.all_gather(latent, 'send', axis=0, tiled=True)]
    ppermute x0 -> x7, starting transfers between devices: none -> 25.8 us  [the longest x3 17.9 us: collect(): later.append(lax.ppermute(later[-1], axis, down))]
    ppermute x0 -> x7, waiting for transfers between devices: none -> 23 us  [the longest x4 21.4 us: collect(): earlier.append(lax.ppermute(earlier[-1], axis, up))]
    all_gather x1, waiting for transfers between devices: 18.9 us -> 0.71 us  [shards(): sender_table = lax.all_gather(latent, 'recv', axis=0, tiled=True)]
  transfers between devices with their start and end apart: 5 -> 11, of which waited for: 5 -> 9; matrix products, arithmetic and copies ran while one was open for 1% -> 2% of each run, Pallas kernels for 0% -> 0%
where the time goes in v1:
time: 627 us; the launch traced here: 624 us
  blocking collectives  269 us (43%)
  waiting for transfers between devices  219 us (35%)
  other arithmetic  38.4 us (6%)
  matrix products  29.9 us (5%)
  starting transfers between devices  26 us (4%)
  local copies, waits for them, and re-layouts  24.4 us (4%)
  between operations  14.6 us (2%)
    psum x1, blocking collectives, shards(): lax.psum((first_grad, second_grad, small_grads), ('recv', 'send'))  269 us
    psum x1, waiting for transfers between devices, shards(): lax.psum((first_grad, second_grad, small_grads), ('recv', 'send'))  101 us
    reduce_scatter x1, waiting for transfers between devices, shards(): lax.psum_scatter(receiver_acc, 'send', scatter_dimension=0, tiled=True)  72.2 us
    ppermute x4, waiting for transfers between devices, collect(): earlier.append(lax.ppermute(earlier[-1], axis, up))  21.4 us
    reduce_scatter x1, waiting for transfers between devices, shards(): lax.psum_scatter(sender_acc, 'recv', scatter_dimension=0, tiled=True)  20.7 us
    ppermute x3, starting transfers between devices, collect(): later.append(lax.ppermute(later[-1], axis, down))  17.9 us
    dot_general x4, matrix products, outer_sum(): lax.dot_general(left, right, (((0,), (0,)), ((), ())), precision=lax.Prec...  13.6 us
  transfers between devices with their start and end apart: 11, of which 9 were waited for; matrix products, arithmetic and copies ran while one was open for 2% of the time, Pallas kernels for 0%

profile of v1, /device:TPU:0, one launch (start us, length us, event | category | flops | bytes accessed | tf_op | source)
XLA Modules:
  0.0 623.8 jit_solution(14411121736397410155)
XLA Ops:
  7.2 3.0 collective-permute-start
  10.2 9.6 %collective-permute-done = f32[128,512]{1,0:T(8,128)S(1)} collective-permute-done((f32[128,512]{1,0:T(8,128)}, f32[128,512]{1,0:T(8,128)S(1)}, u32[]{:S(2)}, u32[]{:S(2)}) %collective-permute-start) | collective-permute-done | bytes 262176 | tf_op jit(solution)/shard_map/ppermute | solution.py:17
  19.8 4.7 collective-permute-start.4
  24.5 6.2 collective-permute-done.1
  30.7 2.5 collective-permute-start.2
  33.2 6.7 %collective-permute-start.5 = (f32[128,512]{1,0:T(8,128)S(1)}, f32[128,512]{1,0:T(8,128)S(1)}, u32[]{:S(2)}, u32[]{:S(2)}) collective-permute-start(f32[128,512]{1,0:T(8,128)S(1)} %collective-permute-done.4), channel_id=1, source_target_pairs={{0,7},{1,0},{2,1},{3,2},{4,3},{5,4},{6,5},{7,6},{8,15},{9,8},{10,9... | collective-permute-start | bytes 786440 | tf_op jit(solution)/shard_map/ppermute | solution.py:19
  39.9 3.3 collective-permute-done.2
  43.2 2.5 collective-permute-start.3
  47.2 6.5 %collective-permute-start.6 = (f32[128,512]{1,0:T(8,128)S(1)}, f32[128,512]{1,0:T(8,128)S(1)}, u32[]{:S(2)}, u32[]{:S(2)}) collective-permute-start(f32[128,512]{1,0:T(8,128)S(1)} %collective-permute-done.5), channel_id=1, source_target_pairs={{0,7},{1,0},{2,1},{3,2},{4,3},{5,4},{6,5},{7,6},{8,15},{9,8},{10,9... | collective-permute-start | bytes 786440 | tf_op jit(solution)/shard_map/ppermute | solution.py:19
  53.6 2.3 collective-permute-done.3
  57.1 1.6 collective-permute-done.6
  58.9 1.5 constant_dynamic-slice_fusion.1
  61.2 1.1 broadcast.81.clone
  63.4 1.6 broadcast.82.clone
  65.0 1.6 broadcast.82
  66.6 2.1 broadcast_in_dim.38
  68.7 77.4 %while.26 = (s32[]{:T(128)}, f32[1536,512]{1,0:T(8,128)}, f32[512,512]{1,0:T(8,128)}, f32[512]{0:T(512)S(1)}, f32[512]{0:T(512)S(1)}, /*index=5*/f32[512]{0:T(51...) while((s32[]{:T(128)}, f32[1536,512]{1,0:T(8,128)}, ...), condition=%wide.region_11.12_spmd, body=%wide.region_0.11_spmd.sunk | while | flops 4836823040 | bytes 46203364 | solution.py:154
  69.7 3.2 gather_fusion
  74.0 2.9 gather_fusion.1
  76.8 1.2 broadcast_select_fusion.5
  78.1 1.9 convolution_add_fusion.7
  81.0 1.2 multiply_reduce_fusion.7
  82.2 1.1 fusion.60
  83.4 1.2 fusion.61
  84.7 1.2 convolution_add_fusion.9
  86.8 4.2 fusion.62
  91.1 4.0 scatter_custom_fusion.11
  95.0 1.8 fusion.63
  96.9 4.7 scatter_custom_fusion.10
  101.5 5.6 convolution_add_fusion.8
  108.0 3.2 gather_fusion
  112.2 2.9 gather_fusion.1
  115.1 1.2 broadcast_select_fusion.5
  116.4 1.9 convolution_add_fusion.7
  119.3 1.2 multiply_reduce_fusion.7
  121.7 1.2 fusion.61
  122.9 1.2 convolution_add_fusion.9
  125.1 4.2 fusion.62
  129.4 4.0 scatter_custom_fusion.11
  133.3 1.8 fusion.63
  135.1 4.7 scatter_custom_fusion.10
  139.8 5.6 convolution_add_fusion.8
  147.4 268.7 %psum.23 = f32[4,512]{1,0:T(4,128)S(1)} all-reduce(f32[4,512]{1,0:T(4,128)S(1)} %pad_maximum_fusion.3), channel_id=1, replica_groups=mesh['recv'=4,'send'=8] {'recv','send'}, use_global_device_ids=true, to_apply=%region_16.17 | all-reduce | flops 2048 | bytes 16384 | tf_op jit(solution)/shard_map/psum | solution.py:161
  416.7 101.5 %all-reduce.3.cloned.1.call-done = (f32[1536,512]{1,0:T(8,128)}, f32[512,512]{1,0:T(8,128)}) async-done(((f32[1536,512]{1,0:T(8,128)}, f32[512,512]{1,0:T(8,128)}), (f32[1536,512]{1,0:T(8,128)}, f32[512,512]{1,0:T(8,128)})) %all-reduce.3.cloned.1.call-update) | async-done | bytes 4194320 | tf_op jit(solution)/shard_map/psum | solution.py:161
  518.2 2.3 broadcast_multiply_fusion.4
  520.5 3.9 broadcast_multiply_fusion.3
  524.4 20.7 %reduce-scatter.3.cloned.1.call-done = f32[128,512]{1,0:T(8,128)} async-done(((f32[512,512]{1,0:T(8,128)}), f32[128,512]{1,0:T(8,128)}) %reduce-scatter.3.cloned.1.call-update) | async-done | bytes 262160 | tf_op jit(solution)/shard_map/reduce_scatter | solution.py:158
  545.1 72.2 %reduce-scatter.5.cloned.1.call-done = f32[128,512]{1,0:T(8,128)} async-done(((f32[1024,512]{1,0:T(8,128)}), f32[128,512]{1,0:T(8,128)}) %reduce-scatter.5.cloned.1.call-update) | async-done | bytes 262160 | tf_op jit(solution)/shard_map/reduce_scatter | solution.py:159
  (101 shorter events, 13.5 us)
Async XLA Ops:
  7.2 51.6 %copy-start.7 = (f32[128,512]{1,0:T(8,128)S(1)}, f32[128,512]{1,0:T(8,128)}, u32[]{:S(2)}) copy-start(f32[128,512]{1,0:T(8,128)} %param.13) | copy-start | bytes 786436
  7.2 54.0 %all-gather.2.cloned.1.call-start = ((), (), s32[]{:S(2)}) async-start(), calls=%async_computation.2 | async-start | bytes 1310720 | tf_op jit(solution)/shard_map/all_gather | solution.py:71
  7.2 12.6 %collective-permute-start = (f32[128,512]{1,0:T(8,128)}, f32[128,512]{1,0:T(8,128)S(1)}, u32[]{:S(2)}, u32[]{:S(2)}) collective-permute-start(f32[128,512]{1,0:T(8,128)} %param.13), channel_id=1, source_target_pairs={{0,1},{1,2},{2,3},{3,4},{4,5},{5,6},{6,7},{7,0},{8,9},{9,10},{10,1... | collective-permute-start | bytes 786440 | tf_op jit(solution)/shard_map/ppermute | solution.py:17
  19.8 10.9 %collective-permute-start.1 = (f32[128,512]{1,0:T(8,128)S(1)}, f32[128,512]{1,0:T(8,128)S(1)}, u32[]{:S(2)}, u32[]{:S(2)}) collective-permute-start(f32[128,512]{1,0:T(8,128)S(1)} %collective-permute-done), channel_id=1, source_target_pairs={{0,1},{1,2},{2,3},{3,4},{4,5},{5,6},{6,7},{7,0},{8,9},{9,10},{10,1... | collective-permute-start | bytes 786440 | tf_op jit(solution)/shard_map/ppermute | solution.py:17
  19.8 13.4 %collective-permute-start.4 = (f32[128,512]{1,0:T(8,128)}, f32[128,512]{1,0:T(8,128)S(1)}, u32[]{:S(2)}, u32[]{:S(2)}) collective-permute-start(f32[128,512]{1,0:T(8,128)} %param.13), channel_id=1, source_target_pairs={{0,7},{1,0},{2,1},{3,2},{4,3},{5,4},{6,5},{7,6},{8,15},{9,8},{10,9... | collective-permute-start | bytes 786440 | tf_op jit(solution)/shard_map/ppermute | solution.py:19
  30.7 12.5 %collective-permute-start.2 = (f32[128,512]{1,0:T(8,128)S(1)}, f32[128,512]{1,0:T(8,128)S(1)}, u32[]{:S(2)}, u32[]{:S(2)}) collective-permute-start(f32[128,512]{1,0:T(8,128)S(1)} %collective-permute-done.1), channel_id=1, source_target_pairs={{0,1},{1,2},{2,3},{3,4},{4,5},{5,6},{6,7},{7,0},{8,9},{9,10},{10,1... | collective-permute-start | bytes 786440 | tf_op jit(solution)/shard_map/ppermute | solution.py:17
  33.2 14.0 %collective-permute-start.5 = (f32[128,512]{1,0:T(8,128)S(1)}, f32[128,512]{1,0:T(8,128)S(1)}, u32[]{:S(2)}, u32[]{:S(2)}) collective-permute-start(f32[128,512]{1,0:T(8,128)S(1)} %collective-permute-done.4), channel_id=1, source_target_pairs={{0,7},{1,0},{2,1},{3,2},{4,3},{5,4},{6,5},{7,6},{8,15},{9,8},{10,9... | collective-permute-start | bytes 786440 | tf_op jit(solution)/shard_map/ppermute | solution.py:19
  43.2 12.7 %collective-permute-start.3 = (f32[128,512]{1,0:T(8,128)S(1)}, f32[128,512]{1,0:T(8,128)S(1)}, u32[]{:S(2)}, u32[]{:S(2)}) collective-permute-start(f32[128,512]{1,0:T(8,128)S(1)} %collective-permute-done.2), channel_id=1, source_target_pairs={{0,1},{1,2},{2,3},{3,4},{4,5},{5,6},{6,7},{7,0},{8,9},{9,10},{10,1... | collective-permute-start | bytes 786440 | tf_op jit(solution)/shard_map/ppermute | solution.py:17
  45.7 472.4 %all-reduce.3.cloned.1.call-start = ((), (), s32[]{:S(2)}) async-start(), calls=%async_computation.5 | async-start | bytes 8388608 | tf_op jit(solution)/shard_map/psum | solution.py:161
  47.2 11.5 %collective-permute-start.6 = (f32[128,512]{1,0:T(8,128)S(1)}, f32[128,512]{1,0:T(8,128)S(1)}, u32[]{:S(2)}, u32[]{:S(2)}) collective-permute-start(f32[128,512]{1,0:T(8,128)S(1)} %collective-permute-done.5), channel_id=1, source_target_pairs={{0,7},{1,0},{2,1},{3,2},{4,3},{5,4},{6,5},{7,6},{8,15},{9,8},{10,9... | collective-permute-start | bytes 786440 | tf_op jit(solution)/shard_map/ppermute | solution.py:19
  62.3 6.4 %copy-start = (f32[1536,512]{1,0:T(8,128)S(1)}, f32[1536,512]{1,0:T(8,128)}, u32[]{:S(2)}) copy-start(f32[1536,512]{1,0:T(8,128)} %param.19) | copy-start | bytes 9437188
  62.3 6.4 %copy-start.8 = (f32[512]{0:T(512)S(1)}, f32[512]{0:T(512)}, u32[]{:S(2)}) copy-start(f32[512]{0:T(512)} %param.23) | copy-start | bytes 6148
  62.3 6.4 %copy-start.9 = (f32[512]{0:T(512)S(1)}, f32[512]{0:T(512)}, u32[]{:S(2)}) copy-start(f32[512]{0:T(512)} %param.20) | copy-start | bytes 6148
  62.3 6.4 %copy-start.10 = (f32[512]{0:T(512)S(1)}, f32[512]{0:T(512)}, u32[]{:S(2)}) copy-start(f32[512]{0:T(512)} %param.22) | copy-start | bytes 6148
  73.9 6.9 %copy-start.2 = (f32[128,512]{1,0:T(8,128)}, f32[128,512]{1,0:T(8,128)S(1)}, u32[]{:S(2)}) copy-start(f32[128,512]{1,0:T(8,128)S(1)} %broadcast_select_fusion.4) | copy-start | bytes 786436 | tf_op jit(solution)/shard_map/while
  76.8 3.1 copy-start.1
  78.1 6.6 %copy-start.3 = (f32[128,512]{1,0:T(8,128)}, f32[128,512]{1,0:T(8,128)S(1)}, u32[]{:S(2)}) copy-start(f32[128,512]{1,0:T(8,128)S(1)} %get-tuple-element.369) | copy-start | bytes 786436 | tf_op jit(solution)/shard_map/while
  78.1 6.6 %copy-start.4 = (f32[128,512]{1,0:T(8,128)}, f32[128,512]{1,0:T(8,128)S(1)}, u32[]{:S(2)}) copy-start(f32[128,512]{1,0:T(8,128)S(1)} %get-tuple-element.370) | copy-start | bytes 786436 | tf_op jit(solution)/shard_map/while
  78.1 6.6 %copy-start.5 = (f32[512,512]{1,0:T(8,128)S(1)}, f32[512,512]{1,0:T(8,128)}, u32[]{:S(2)}) copy-start(f32[512,512]{1,0:T(8,128)} %get-tuple-element.411) | copy-start | bytes 3145732 | tf_op jit(solution)/shard_map/while
  85.9 1.0 copy-start.6
  112.2 6.9 %copy-start.2 = (f32[128,512]{1,0:T(8,128)}, f32[128,512]{1,0:T(8,128)S(1)}, u32[]{:S(2)}) copy-start(f32[128,512]{1,0:T(8,128)S(1)} %broadcast_select_fusion.4) | copy-start | bytes 786436 | tf_op jit(solution)/shard_map/while
  115.1 3.1 copy-start.1
  116.3 6.6 %copy-start.3 = (f32[128,512]{1,0:T(8,128)}, f32[128,512]{1,0:T(8,128)S(1)}, u32[]{:S(2)}) copy-start(f32[128,512]{1,0:T(8,128)S(1)} %get-tuple-element.369) | copy-start | bytes 786436 | tf_op jit(solution)/shard_map/while
  116.3 6.6 %copy-start.4 = (f32[128,512]{1,0:T(8,128)}, f32[128,512]{1,0:T(8,128)S(1)}, u32[]{:S(2)}) copy-start(f32[128,512]{1,0:T(8,128)S(1)} %get-tuple-element.370) | copy-start | bytes 786436 | tf_op jit(solution)/shard_map/while
  116.3 6.6 %copy-start.5 = (f32[512,512]{1,0:T(8,128)S(1)}, f32[512,512]{1,0:T(8,128)}, u32[]{:S(2)}) copy-start(f32[512,512]{1,0:T(8,128)} %get-tuple-element.411) | copy-start | bytes 3145732 | tf_op jit(solution)/shard_map/while
  124.1 1.0 copy-start.6
  146.1 399.0 %reduce-scatter.3.cloned.1.call-start = ((), (), s32[]{:S(2)}) async-start(), calls=%async_computation.3 | async-start | bytes 1310720 | tf_op jit(solution)/shard_map/reduce_scatter | solution.py:158
  146.8 470.4 %reduce-scatter.5.cloned.1.call-start = ((), (), s32[]{:S(2)}) async-start(), calls=%async_computation.4 | async-start | bytes 2359296 | tf_op jit(solution)/shard_map/reduce_scatter | solution.py:159
Sparse Core Ops, SparseCore 0:
  45.8 15.2 all-gather.1
  146.2 371.8 all-reduce.2
  521.3 23.7 reduce-scatter.2
  549.4 67.7 reduce-scatter.4
